TPU v7x, 256 devices: a whole 4x4x8 slice. The times are simulated.
256 devices in a mesh: rows: 4 (over y), coarse: 4 (over x_lo, core), fine: 16 (over z, x_hi).
Axes of the slice: x: 4 (x_hi: 2, x_lo: 2; x = x_hi * 2 + x_lo), y: 4, z: 8, core: 2. Of those that a mesh axis runs over, the one named last changes fastest.
Arguments:
- eigvecs: bfloat16 [2048, 32768], P('rows', ('coarse', 'fine')), may hold values from -6 to 6
- perm: int32 [32768], P(('coarse', 'fine')), may hold values from 0 to 511, as said below
- counts: int32 [64], replicated, may hold values from 1 to 256, as said below
- poles: float32 [32768], replicated, may hold values from 0 to 32768, as said below
- weights: float32 [32768], replicated, may hold values from -10 to 10, as said below
- roots: float32 [32768], P(('coarse', 'fine')), may hold values from 0 to 32768, as said below
Outputs:
- merged: bfloat16 [2048, 32768], P('rows', ('coarse', 'fine'))
Inputs may be any that keep to these rules, and one draw needn't show every extreme that they name: `perm`: each aligned block of 512 entries is a permutation of 0 to 511. `counts`: at least one device has exactly 256. Every entry of poles lies 0.2 or more away from every entry of roots. `weights`: magnitudes 0.1 or more. `roots`: every entry lies 0.2 or more away from every entry of poles.
All inputs are finite; a program needn't handle non-finite values.
Results may differ from a plain program's by a relative error of at most 0.0027.
Values may be sent and summed in bfloat16 or wider, within the bound.
No kernel may reach another device: no remote copies, remote signals or barrier semaphores. Data moves between devices by JAX's collectives and lax.ppermute only.
A program may use at most 64 MiB of HBM per device.

v0:
```python
import jax
import jax.numpy as jnp
from jax import lax
from jax.sharding import PartitionSpec as P

UNDEF_MOST = 256


def per_device(eigvecs, perm, counts, poles, weights, roots):
    columns_dev = eigvecs.shape[1]
    live_width = UNDEF_MOST
    device_total = counts.shape[0]
    n_coarse = lax.axis_size("coarse")
    n_fine = lax.axis_size("fine")
    device_ids = jnp.arange(device_total, dtype=jnp.int32)
    my_device = lax.axis_index("coarse") * n_fine + lax.axis_index("fine")
    my_count = jnp.sum(jnp.where(device_ids == my_device, counts, 0))
    column_ids = jnp.arange(columns_dev, dtype=jnp.int32)
    selector = (column_ids[:, None] == perm[None, :]).astype(jnp.bfloat16)
    permuted = jnp.dot(eigvecs, selector, preferred_element_type=jnp.float32).astype(jnp.bfloat16)
    own_roots = roots[:live_width]
    outgoing = permuted[:, :live_width]
    within = jnp.arange(live_width, dtype=jnp.int32)
    alive = within[None, :] < counts[:, None]
    factor_table = jnp.where(alive, weights.reshape(device_total, columns_dev)[:, :live_width], 0.0)
    pole_table = poles.reshape(device_total, columns_dev)[:, :live_width]
    factor_flat = jnp.transpose(
        factor_table.reshape(n_coarse, n_fine, live_width), (1, 0, 2)
    ).reshape(-1)
    pole_flat = jnp.transpose(pole_table.reshape(n_coarse, n_fine, live_width), (1, 0, 2)).reshape(
        -1
    )
    panels = lax.all_gather(outgoing, "coarse", axis=1, tiled=True)
    panel_piece = lax.all_gather(panels, "fine", axis=1, tiled=True)
    cauchy = factor_flat[:, None] / (pole_flat[:, None] - own_roots[None, :])
    summed = jnp.dot(panel_piece, cauchy.astype(jnp.bfloat16), preferred_element_type=jnp.float32)
    summed, squares = (summed, jnp.sum(cauchy * cauchy, axis=0))
    updated = summed / jnp.sqrt(squares)[None, :]
    retain = within < my_count
    leading = jnp.where(retain[None, :], updated, outgoing.astype(jnp.float32)).astype(jnp.bfloat16)
    return jnp.concatenate([leading, permuted[:, live_width:]], axis=1)


def solution(mesh):
    in_specs = (
        P("rows", ("coarse", "fine")),
        P(("coarse", "fine")),
        P(),
        P(),
        P(),
        P(("coarse", "fine")),
    )
    out_specs = P("rows", ("coarse", "fine"))
    return jax.shard_map(
        per_device, mesh=mesh, in_specs=in_specs, out_specs=out_specs, check_vma=False
    )
```

profile of v0, /device:TPU:1, one launch (start us, length us, event | category | flops | bytes accessed | tf_op | source)
XLA Modules:
  0.0 287.3 jit_solution(11880553413928689479)
XLA Ops:
  6.5 0.0 copy-start
  6.5 0.0 all-gather.3.cloned.1.call-start
  6.5 1.0 copy-done
  7.6 1.2 fusion.6
  8.8 0.7 fusion.20
  9.5 0.0 all-gather.3.cloned.1.call-update
  9.5 0.0 all-gather.5.cloned.1.call-start
  9.6 27.6 %all-gather.3.cloned.1.call-done = bf16[512,1024]{0,1:T(8,128)(2,1)} async-done(((bf16[512,256]{0,1:T(8,128)(2,1)}), bf16[512,1024]{0,1:T(8,128)(2,1)}) %all-gather.3.cloned.1.call-update) | async-done | bytes 1048592 | tf_op jit(solution)/shard_map/all_gather | solution.py:33
  37.1 0.0 all-gather.5.cloned.1.call-update
  37.1 0.7 slice.18
  37.8 0.9 reshape.26
  38.9 0.9 reshape.24
  39.8 0.7 slice_select_fusion
  40.6 9.0 %multiply_reduce_fusion = f32[256]{0:T(256)S(1)} fusion(f32[256]{0:T(256)S(1)} %slice.18, f32[16384]{0:T(1024)S(1)} %bitcast.18, f32[16384]{0:T(1024)S(1)} %bitcast.20), kind=kLoop, calls=%fused_computation | loop fusion | flops 16776960 | bytes 133120 | tf_op jit(solution)/shard_map/reduce_sum | solution.py:37
  49.7 1.3 fusion.19
  51.0 0.6 iota_compare_fusion.2
  51.6 213.3 %all-gather.5.cloned.1.call-done = bf16[512,16384]{0,1:T(8,128)(2,1)} async-done(((bf16[512,1024]{0,1:T(8,128)(2,1)}), bf16[512,16384]{0,1:T(8,128)(2,1)}) %all-gather.5.cloned.1.call-update) | async-done | bytes 16777232 | tf_op jit(solution)/shard_map/all_gather | solution.py:34
  264.9 14.5 %fusion.13 = bf16[512,256]{0,1:T(8,128)(2,1)S(1)} fusion(bf16[512,16384]{0,1:T(8,128)(2,1)} %all-gather.5.cloned.1.call-done, f32[256]{0:T(256)S(1)} %slice.18, f32[16384]{0:T(1024)S(1)} %bitcast.19, f32[16384]{0:T(1024)S(1)} %bitcast.21, f32[256]{0:T(256)S(1)} %sqrt.7, pred[256]{0:T(512)(128)(4,1)S(1)} %iota_compare_fusion.2, bf16[512,512]{0,1:T(8,128)(2,1)S(1)} %fusion.6), kind=kOutput, calls=%fused_computation.11 | convolution fusion | flops 4308074496 | bytes 17434880 | tf_op jit(solution)/shard_map/dot_general | solution.py:36
  279.5 1.0 copy.14
  (7 shorter events, 0.2 us)
Async XLA Ops:
  6.5 1.0 copy-start
  6.5 30.6 %all-gather.3.cloned.1.call-start = ((), (), s32[]{:S(2)}) async-start(), calls=%async_computation | async-start | bytes 1310720 | tf_op jit(solution)/shard_map/all_gather | solution.py:33
  9.5 255.4 %all-gather.5.cloned.1.call-start = ((), (), s32[]{:S(2)}) async-start(), calls=%async_computation.1 | async-start | bytes 17825792 | tf_op jit(solution)/shard_map/all_gather | solution.py:34
Sparse Core Ops, SparseCore 0:
  9.6 27.4 all-gather.2
  39.7 225.1 all-gather.4
where the time goes:
time: 288 us; the launch traced here: 287 us
  waiting for transfers between devices  241 us (84%)
  matrix products  15.7 us (5%)
  between operations  13.5 us (5%)
  other arithmetic  11.7 us (4%)
  local copies, waits for them, and re-layouts  5.5 us (2%)
    all_gather x1, waiting for transfers between devices, per_device(): panel_piece = lax.all_gather(panels, 'fine', axis=1, tiled=True)  213 us
    all_gather x1, waiting for transfers between devices, per_device(): panels = lax.all_gather(outgoing, 'coarse', axis=1, tiled=True)  27.6 us
    dot_general x1, matrix products, per_device(): jnp.dot(panel_piece, cauchy.astype(jnp.bfloat16), preferred_element_type=...  14.5 us
    reduce_sum x1, other arithmetic, per_device(): summed, squares = (summed, jnp.sum(cauchy * cauchy, axis=0))  9.01 us
  transfers between devices with their start and end apart: 2, of which 2 were waited for; matrix products, arithmetic and copies ran while one was open for 5% of the time, Pallas kernels for 0%

commit v1 on v0

--- a/solution.py
+++ b/solution.py
@@ -30,7 +30,8 @@
     pole_flat = jnp.transpose(pole_table.reshape(n_coarse, n_fine, live_width), (1, 0, 2)).reshape(
         -1
     )
-    panels = lax.all_gather(outgoing, "coarse", axis=1, tiled=True)
+    outgoing_2 = jnp.stack([outgoing] * lax.axis_size("coarse"))
+    panels = jnp.concatenate(lax.all_to_all(outgoing_2, "coarse", 0, 0), axis=1)
     panel_piece = lax.all_gather(panels, "fine", axis=1, tiled=True)
     cauchy = factor_flat[:, None] / (pole_flat[:, None] - own_roots[None, :])
     summed = jnp.dot(panel_piece, cauchy.astype(jnp.bfloat16), preferred_element_type=jnp.float32)

time: 288 us -> 278 us (0.965)
  waiting for transfers between devices: 241 us -> 212 us
  blocking collectives: 0 us -> 19.8 us
    all_gather x1 -> x0, waiting for transfers between devices: 27.6 us -> none  [per_device(): panels = lax.all_gather(outgoing, 'coarse', axis=1, tiled=True)]
    all_to_all x0 -> x1, blocking collectives: none -> 19.8 us  [per_device(): panels = jnp.concatenate(lax.all_to_all(outgoing_2, 'coarse', 0, 0), axis=1)]
  transfers between devices with their start and end apart: 2 -> 1, of which waited for: 2 -> 1; matrix products, arithmetic and copies ran while one was open for 5% -> 5% of each run, Pallas kernels for 0% -> 0%
where the time goes in v1:
time: 278 us; the launch traced here: 277 us
  waiting for transfers between devices  212 us (76%)
  blocking collectives  19.8 us (7%)
  matrix products  15.7 us (6%)
  between operations  13.5 us (5%)
  other arithmetic  11.7 us (4%)
  local copies, waits for them, and re-layouts  4.88 us (2%)
    all_gather x1, waiting for transfers between devices, per_device(): panel_piece = lax.all_gather(panels, 'fine', axis=1, tiled=True)  212 us
    all_to_all x1, blocking collectives, per_device(): panels = jnp.concatenate(lax.all_to_all(outgoing_2, 'coarse', 0, 0), axis=1)  19.8 us
    dot_general x1, matrix products, per_device(): jnp.dot(panel_piece, cauchy.astype(jnp.bfloat16), preferred_element_type=...  14.5 us
    reduce_sum x1, other arithmetic, per_device(): summed, squares = (summed, jnp.sum(cauchy * cauchy, axis=0))  9.01 us
  transfers between devices with their start and end apart: 1, of which 1 were waited for; matrix products, arithmetic and copies ran while one was open for 5% of the time, Pallas kernels for 0%

profile of v1, /device:TPU:1, one launch (start us, length us, event | category | flops | bytes accessed | tf_op | source)
XLA Modules:
  0.0 277.5 jit_solution(8673869450973481017)
XLA Ops:
  6.5 0.0 copy-start
  6.5 0.0 all-gather.2.cloned.1.call-start
  6.5 1.0 copy-done
  7.6 1.2 fusion.6
  8.8 0.1 stack.2
  8.9 19.8 %all_to_all.5 = bf16[4,512,256]{1,2,0:T(8,128)(2,1)} all-to-all(bf16[4,512,256]{1,2,0:T(8,128)(2,1)S(1)} %stack.2), channel_id=1, replica_groups=mesh['rows'=4,'coarse'=4,'fine'=16] {'coarse'}, dimensions={0} | all-to-all | bytes 2097152 | tf_op jit(solution)/shard_map/all_to_all | solution.py:34
  28.7 0.0 all-gather.2.cloned.1.call-update
  28.7 0.7 slice.18
  29.4 0.9 reshape.36
  30.4 0.9 reshape.34
  31.4 0.7 slice_select_fusion
  32.2 9.0 %multiply_reduce_fusion = f32[256]{0:T(256)S(1)} fusion(f32[256]{0:T(256)S(1)} %slice.18, f32[16384]{0:T(1024)S(1)} %bitcast.22, f32[16384]{0:T(1024)S(1)} %bitcast.24), kind=kLoop, calls=%fused_computation | loop fusion | flops 16776960 | bytes 133120 | tf_op jit(solution)/shard_map/reduce_sum | solution.py:38
  41.2 1.3 fusion.19
  42.5 0.7 iota_compare_fusion.2
  43.2 211.9 %all-gather.2.cloned.1.call-done = bf16[512,16384]{0,1:T(8,128)(2,1)} async-done(((bf16[512,1024]{0,1:T(8,128)(2,1)}), bf16[512,16384]{0,1:T(8,128)(2,1)}) %all-gather.2.cloned.1.call-update) | async-done | bytes 16777232 | tf_op jit(solution)/shard_map/all_gather | solution.py:35
  255.1 14.5 %fusion.13 = bf16[512,256]{0,1:T(8,128)(2,1)S(1)} fusion(bf16[512,16384]{0,1:T(8,128)(2,1)} %all-gather.2.cloned.1.call-done, f32[256]{0:T(256)S(1)} %slice.18, f32[16384]{0:T(1024)S(1)} %bitcast.23, f32[16384]{0:T(1024)S(1)} %bitcast.25, f32[256]{0:T(256)S(1)} %sqrt.7, pred[256]{0:T(512)(128)(4,1)S(1)} %iota_compare_fusion.2, bf16[512,512]{0,1:T(8,128)(2,1)S(1)} %fusion.6), kind=kOutput, calls=%fused_computation.11 | convolution fusion | flops 4308074496 | bytes 17434880 | tf_op jit(solution)/shard_map/dot_general | solution.py:37
  269.6 1.0 copy.15
  (8 shorter events, 0.2 us)
Async XLA Ops:
  6.5 1.0 copy-start
  6.5 248.6 %all-gather.2.cloned.1.call-start = ((), (), s32[]{:S(2)}) async-start(), calls=%async_computation.1 | async-start | bytes 17825792 | tf_op jit(solution)/shard_map/all_gather | solution.py:35
Sparse Core Ops, SparseCore 0:
  28.8 226.2 all-gather.1
